TPU v7x, 32 devices: a whole 2x2x4 slice. The times are simulated.
32 devices in a mesh: tensor: 4 (over z), group: 4 (over y, core), cross: 2 (over x).
Axes of the slice: x: 2, y: 2, z: 4, core: 2. Of those that a mesh axis runs over, the one named last changes fastest.
Arguments:
- inputs: bfloat16 [16, 1568, 1024], P(('group', 'cross'), 'tensor'), may hold values from -6 to 6
- clips_here: int32 [8], P(('group', 'cross')), may hold values from 1 to 2, as said below
- first_gain: bfloat16 [1024], replicated, may hold values from 0.5 to 1.5
- first_shift: bfloat16 [1024], replicated, may hold values from -1.25 to 1.25
- query_key_value: bfloat16 [3, 1024, 1024], P(None, 'group', 'tensor'), may hold values from -0.1875 to 0.1875
- query_bias: bfloat16 [1024], P('tensor'), may hold values from -3 to 3
- value_bias: bfloat16 [1024], P('tensor'), may hold values from -0.1875 to 0.1875
- output_weight: bfloat16 [1024, 1024], P('tensor', 'group'), may hold values from -6 to 6
- output_bias: bfloat16 [1024], replicated, may hold values from -3 to 3
- second_gain: bfloat16 [1024], replicated, may hold values from 0.5 to 1.5
- second_shift: bfloat16 [1024], replicated, may hold values from -1.25 to 1.25
- expand_weight: bfloat16 [1024, 4096], P('group', 'tensor'), may hold values from -0.1875 to 0.1875
- expand_bias: bfloat16 [4096], P('tensor'), may hold values from -3 to 3
- contract_weight: bfloat16 [4096, 1024], P('tensor', 'group'), may hold values from -0.09375 to 0.09375
- contract_bias: bfloat16 [1024], replicated, may hold values from -3 to 3
- output_grad: bfloat16 [16, 1568, 1024], P(('group', 'cross'), 'tensor'), may hold values from -6 to 6
Outputs:
- output: bfloat16 [16, 1568, 1024], P(('group', 'cross'), 'tensor')
- input_grad: bfloat16 [16, 1568, 1024], P(('group', 'cross'), 'tensor')
- first_gain_grad: float32 [1024], P('group')
- first_shift_grad: float32 [1024], P('group')
- query_key_value_grad: float32 [3, 1024, 1024], P(None, 'group', 'tensor')
- query_bias_grad: float32 [1024], P(('tensor', 'group'))
- value_bias_grad: float32 [1024], P(('tensor', 'group'))
- output_weight_grad: float32 [1024, 1024], P('tensor', 'group')
- output_bias_grad: float32 [1024], P('group')
- second_gain_grad: float32 [1024], P('group')
- second_shift_grad: float32 [1024], P('group')
- expand_weight_grad: float32 [1024, 4096], P('group', 'tensor')
- expand_bias_grad: float32 [4096], P(('tensor', 'group'))
- contract_weight_grad: float32 [4096, 1024], P('tensor', 'group')
- contract_bias_grad: float32 [1024], P('group')
Inputs may be any that keep to these rules, and one draw needn't show every extreme that they name: Exactly half of the 8 data positions hold 2 clips and the others 1; slot p * 2 + j holds a clip if j < clips_here[p].
All inputs are finite; a program needn't handle non-finite values.
Results may differ from a plain program's by a relative error of at most 0.02.
Values may be sent and summed in bfloat16 or wider, within the bound.
A program may use at most 192 MiB of HBM per device.

v0:
```python
import jax
import jax.numpy as jnp
from jax import lax
from jax.sharding import PartitionSpec as P

HEAD = 64
epsilon = 1e-06
root_half = 0.7071067811865476
inv_root_two_pi = 0.3989422804014327


def normalize(values):
    center = values - jnp.mean(values, axis=-1, keepdims=True)
    inverse = lax.rsqrt(jnp.mean(center * center, axis=-1, keepdims=True) + epsilon)
    return (center * inverse, inverse)


def normalize_back(upstream, normed, inverse, norm_gain):
    scaled = upstream * norm_gain
    return inverse * (
        scaled
        - jnp.mean(scaled, axis=-1, keepdims=True)
        - normed * jnp.mean(scaled * normed, axis=-1, keepdims=True)
    )


def attend_forward(triple):
    query_rows, key_rows, value_rows = triple
    length = query_rows.shape[0]
    head_count = query_rows.shape[1] // HEAD
    key_heads = key_rows.reshape(length, head_count, HEAD)
    value_heads = value_rows.reshape(length, head_count, HEAD)
    query_parts = query_rows.reshape(2, length // 2, head_count, HEAD)

    def one_part(query_part):
        logits = jnp.einsum(
            "bhe,lhe->hbl", query_part, key_heads, preferred_element_type=jnp.float32
        ) * HEAD ** (-0.5)
        largest = jnp.max(logits, axis=-1, keepdims=True)
        powers = jnp.exp(logits - largest)
        totals = jnp.sum(powers, axis=-1, keepdims=True)
        probs = (powers / totals).astype(jnp.bfloat16)
        attention_result = jnp.einsum(
            "hbl,lhe->bhe", probs, value_heads, preferred_element_type=jnp.float32
        )
        return (attention_result.astype(jnp.bfloat16), largest + jnp.log(totals))

    attention_result, log_totals = lax.map(one_part, query_parts)
    return (attention_result.reshape(length, head_count * HEAD), log_totals)


def attend_backward(entries):
    query_rows, key_rows, value_rows, upstream_rows, log_totals = entries
    length = query_rows.shape[0]
    head_count = query_rows.shape[1] // HEAD
    key_heads = key_rows.reshape(length, head_count, HEAD)
    value_heads = value_rows.reshape(length, head_count, HEAD)
    query_parts = query_rows.reshape(2, length // 2, head_count, HEAD)
    upstream_parts = upstream_rows.reshape(2, length // 2, head_count, HEAD)

    def one_part(carry, part_items):
        key_grad, value_grad = carry
        query_part, upstream_part, log_total = part_items
        logits = jnp.einsum(
            "bhe,lhe->hbl", query_part, key_heads, preferred_element_type=jnp.float32
        ) * HEAD ** (-0.5)
        probs = jnp.exp(logits - log_total)
        prob_grad = jnp.einsum(
            "bhe,lhe->hbl", upstream_part, value_heads, preferred_element_type=jnp.float32
        )
        inner = jnp.sum(probs * prob_grad, axis=-1, keepdims=True)
        logit_grad = (probs * (prob_grad - inner) * HEAD ** (-0.5)).astype(jnp.bfloat16)
        query_grad = jnp.einsum(
            "hbl,lhe->bhe", logit_grad, key_heads, preferred_element_type=jnp.float32
        )
        key_grad = key_grad + jnp.einsum(
            "hbl,bhe->lhe", logit_grad, query_part, preferred_element_type=jnp.float32
        )
        value_grad = value_grad + jnp.einsum(
            "hbl,bhe->lhe",
            probs.astype(jnp.bfloat16),
            upstream_part,
            preferred_element_type=jnp.float32,
        )
        return ((key_grad, value_grad), query_grad.astype(jnp.bfloat16))

    empty_grad = jnp.zeros((length, head_count, HEAD), jnp.float32)
    (key_grad, value_grad), query_grads = lax.scan(
        one_part, (empty_grad, empty_grad), (query_parts, upstream_parts, log_totals)
    )
    width = head_count * HEAD
    return (
        query_grads.reshape(length, width),
        key_grad.astype(jnp.bfloat16).reshape(length, width),
        value_grad.astype(jnp.bfloat16).reshape(length, width),
    )


def gelu_slope(hidden_pre):
    normal_cdf = 0.5 * (1.0 + lax.erf(hidden_pre * root_half))
    normal_pdf = inv_root_two_pi * jnp.exp(-0.5 * hidden_pre * hidden_pre)
    return normal_cdf + hidden_pre * normal_pdf


def local(
    inputs,
    clips_here,
    first_gain,
    first_shift,
    query_key_value,
    query_bias,
    value_bias,
    output_weight,
    output_bias,
    second_gain,
    second_shift,
    expand_weight,
    expand_bias,
    contract_weight,
    contract_bias,
    output_grad,
):
    floating_kind = jnp.float32
    slot_count = inputs.shape[0]
    tensor_index = lax.axis_index("tensor")
    tensor_count = lax.axis_size("tensor")
    group_index = lax.axis_index("group")
    group_count = lax.axis_size("group")

    def widen(local_vector):
        width = local_vector.shape[0]
        return lax.dynamic_update_slice(
            jnp.zeros((width * tensor_count,), floating_kind), local_vector, (tensor_index * width,)
        )

    alive_mask = (jnp.arange(slot_count, dtype=jnp.int32) < clips_here[0]).astype(floating_kind)[
        :, None, None
    ]
    (
        triple_weight_complete,
        output_weight_complete,
        expand_weight_complete,
        contract_weight_complete,
    ) = (
        lax.all_gather(query_key_value, "group", axis=1, tiled=True),
        lax.all_gather(output_weight, "group", axis=1, tiled=True),
        lax.all_gather(expand_weight, "group", axis=0, tiled=True),
        lax.all_gather(contract_weight, "group", axis=1, tiled=True),
    )
    gain_one = first_gain.astype(floating_kind)
    gain_two = second_gain.astype(floating_kind)
    tokens = inputs.astype(floating_kind)
    first_plain, first_inverse = normalize(tokens)
    first_rows = (first_plain * gain_one + first_shift.astype(floating_kind)).astype(jnp.bfloat16)
    first_gathered = lax.all_gather(first_rows, "tensor", axis=1, tiled=True)
    bias_stack = jnp.stack([query_bias, jnp.zeros_like(query_bias), value_bias]).astype(
        floating_kind
    )
    projected = jnp.einsum(
        "ruh,nhm->nrum",
        first_gathered,
        triple_weight_complete,
        preferred_element_type=floating_kind,
    )
    projected = (projected + bias_stack[:, None, None, :]).astype(jnp.bfloat16)
    attention_result, log_totals = lax.map(
        attend_forward, (projected[0], projected[1], projected[2])
    )
    attention_terms = jnp.einsum(
        "hpx,xj->hpj",
        attention_result,
        output_weight_complete,
        preferred_element_type=floating_kind,
    )
    attention_part = lax.psum_scatter(
        attention_terms.astype(jnp.bfloat16), "tensor", scatter_dimension=1, tiled=True
    ).astype(jnp.float32)
    middle = tokens + attention_part + output_bias.astype(floating_kind)
    second_plain, second_inverse = normalize(middle)
    second_rows = (second_plain * gain_two + second_shift.astype(floating_kind)).astype(
        jnp.bfloat16
    )
    top_grad = output_grad.astype(floating_kind) * alive_mask
    feed_grad = top_grad.astype(jnp.bfloat16)
    contract_bias_part = jnp.sum(feed_grad.astype(floating_kind), axis=(0, 1))
    second_gathered = lax.all_gather(second_rows, "tensor", axis=1, tiled=True)
    hidden_pre = jnp.einsum(
        "njz,zc->njc", second_gathered, expand_weight_complete, preferred_element_type=floating_kind
    )
    hidden_pre = hidden_pre + expand_bias.astype(floating_kind)
    hidden_activation = jax.nn.gelu(hidden_pre, approximate=False).astype(jnp.bfloat16)
    feed_forward_terms = jnp.einsum(
        "ybj,jx->ybx",
        hidden_activation,
        contract_weight_complete,
        preferred_element_type=floating_kind,
    )
    feed_part = lax.psum_scatter(
        feed_forward_terms.astype(jnp.bfloat16), "tensor", scatter_dimension=1, tiled=True
    ).astype(jnp.float32)
    output = (middle + feed_part + contract_bias.astype(floating_kind)).astype(jnp.bfloat16)
    feed_grad_gathered = lax.all_gather(feed_grad, "tensor", axis=1, tiled=True)
    contract_weight_part = jnp.einsum(
        "gct,gcu->tu", hidden_activation, feed_grad_gathered, preferred_element_type=floating_kind
    )
    hidden_grad = jnp.einsum(
        "bxn,qn->bxq",
        feed_grad_gathered,
        contract_weight_complete,
        preferred_element_type=floating_kind,
    )
    preactivation_grad = (hidden_grad * gelu_slope(hidden_pre)).astype(jnp.bfloat16)
    expand_bias_vector = widen(jnp.sum(preactivation_grad.astype(floating_kind), axis=(0, 1)))
    expand_weight_part = jnp.einsum(
        "aew,aex->wx", second_gathered, preactivation_grad, preferred_element_type=floating_kind
    )
    second_terms = jnp.einsum(
        "rci,ei->rce",
        preactivation_grad,
        expand_weight_complete,
        preferred_element_type=floating_kind,
    )
    second_grad = lax.psum_scatter(
        second_terms.astype(jnp.bfloat16), "tensor", scatter_dimension=1, tiled=True
    ).astype(jnp.float32)
    second_gain_part = jnp.sum(second_grad * second_plain, axis=(0, 1))
    second_shift_part = jnp.sum(second_grad, axis=(0, 1))
    middle_grad = top_grad + normalize_back(second_grad, second_plain, second_inverse, gain_two)
    branch_grad = middle_grad.astype(jnp.bfloat16)
    output_bias_part = jnp.sum(branch_grad.astype(floating_kind), axis=(0, 1))
    branch_gathered = lax.all_gather(branch_grad, "tensor", axis=1, tiled=True)
    output_weight_part = jnp.einsum(
        "vat,vah->th", attention_result, branch_gathered, preferred_element_type=floating_kind
    )
    attended_grad = jnp.einsum(
        "ghv,cv->ghc", branch_gathered, output_weight_complete, preferred_element_type=floating_kind
    ).astype(jnp.bfloat16)
    query_grad, key_grad, value_grad = lax.map(
        attend_backward, (projected[0], projected[1], projected[2], attended_grad, log_totals)
    )
    triple_weight_gradient = jnp.stack([query_grad, key_grad, value_grad])
    query_bias_part = jnp.sum(query_grad.astype(floating_kind), axis=(0, 1))
    value_bias_part = jnp.sum(value_grad.astype(floating_kind), axis=(0, 1))
    triple_weight_part = jnp.einsum(
        "ayn,iayf->inf",
        first_gathered,
        triple_weight_gradient,
        preferred_element_type=floating_kind,
    )
    first_terms = jnp.einsum(
        "hpxw,hgw->pxg",
        triple_weight_gradient,
        triple_weight_complete,
        preferred_element_type=floating_kind,
    )
    first_grad = lax.psum_scatter(
        first_terms.astype(jnp.bfloat16), "tensor", scatter_dimension=1, tiled=True
    ).astype(jnp.float32)
    first_gain_part = jnp.sum(first_grad * first_plain, axis=(0, 1))
    first_shift_part = jnp.sum(first_grad, axis=(0, 1))
    input_grad = (
        middle_grad + normalize_back(first_grad, first_plain, first_inverse, gain_one)
    ).astype(jnp.bfloat16)
    large_parts = (triple_weight_part, output_weight_part, expand_weight_part, contract_weight_part)
    group_parts = (
        lax.psum_scatter(
            large_parts[0].astype(jnp.bfloat16), "group", scatter_dimension=1, tiled=True
        ).astype(jnp.float32),
        lax.psum_scatter(
            large_parts[1].astype(jnp.bfloat16), "group", scatter_dimension=1, tiled=True
        ).astype(jnp.float32),
        lax.psum_scatter(
            large_parts[2].astype(jnp.bfloat16), "group", scatter_dimension=0, tiled=True
        ).astype(jnp.float32),
        lax.psum_scatter(
            large_parts[3].astype(jnp.bfloat16), "group", scatter_dimension=1, tiled=True
        ).astype(jnp.float32),
    )
    large_sums = (
        lax.psum(group_parts[0].astype(jnp.bfloat16), "cross").astype(jnp.float32),
        lax.psum(group_parts[1].astype(jnp.bfloat16), "cross").astype(jnp.float32),
        lax.psum(group_parts[2].astype(jnp.bfloat16), "cross").astype(jnp.float32),
        lax.psum(group_parts[3].astype(jnp.bfloat16), "cross").astype(jnp.float32),
    )
    small_sums = lax.psum(
        (
            first_gain_part,
            first_shift_part,
            widen(query_bias_part),
            widen(value_bias_part),
            output_bias_part,
            second_gain_part,
            second_shift_part,
            expand_bias_vector,
            contract_bias_part,
        ),
        ("tensor", "group", "cross"),
    )

    def own_group(full_vector):
        width = full_vector.shape[0] // group_count
        return lax.dynamic_slice_in_dim(full_vector, group_index * width, width)

    def own_split(full_vector):
        width = full_vector.shape[0] // (group_count * tensor_count)
        return lax.dynamic_slice_in_dim(
            full_vector, (tensor_index * group_count + group_index) * width, width
        )

    return (
        output,
        input_grad,
        own_group(small_sums[0]),
        own_group(small_sums[1]),
        large_sums[0],
        own_split(small_sums[2]),
        own_split(small_sums[3]),
        large_sums[1],
        own_group(small_sums[4]),
        own_group(small_sums[5]),
        own_group(small_sums[6]),
        large_sums[2],
        own_split(small_sums[7]),
        large_sums[3],
        own_group(small_sums[8]),
    )


def solution(mesh):
    in_specs = (
        P(("group", "cross"), "tensor", None),
        P(("group", "cross")),
        P(),
        P(),
        P(None, "group", "tensor"),
        P("tensor"),
        P("tensor"),
        P("tensor", "group"),
        P(),
        P(),
        P(),
        P("group", "tensor"),
        P("tensor"),
        P("tensor", "group"),
        P(),
        P(("group", "cross"), "tensor", None),
    )
    out_specs = (
        P(("group", "cross"), "tensor", None),
        P(("group", "cross"), "tensor", None),
        P("group"),
        P("group"),
        P(None, "group", "tensor"),
        P(("tensor", "group")),
        P(("tensor", "group")),
        P("tensor", "group"),
        P("group"),
        P("group"),
        P("group"),
        P("group", "tensor"),
        P(("tensor", "group")),
        P("tensor", "group"),
        P("group"),
    )
    return jax.shard_map(local, mesh=mesh, in_specs=in_specs, out_specs=out_specs, check_vma=False)
```

profile of v0, /device:TPU:0, one launch (start us, length us, event | category | flops | bytes accessed | tf_op | source)
XLA Modules:
  0.0 1773.0 jit_solution(4338053443137835705)
XLA Ops:
  15.8 10.8 all_gather.26
  33.5 120.5 %all-gather.8.cloned.1.call-done = bf16[2,1568,1024]{2,1,0:T(8,128)(2,1)} async-done(((bf16[2,392,1024]{2,1,0:T(8,128)(2,1)}), bf16[2,1568,1024]{2,1,0:T(8,128)(2,1)}) %all-gather.8.cloned.1.call-update) | async-done | bytes 6422544 | tf_op jit(solution)/shard_map/all_gather | solution.py:155
  154.0 7.8 fusion.79
  173.9 81.3 %while.54 = (s32[]{:T(128)}, bf16[2,1568,256]{1,2,0:T(8,128)(2,1)}, f32[2,2,4,784,1]{3,2,1,4,0:T(4,128)}, bf16[2,1568,256]{1,2,0:T(8,128)(2,1)}, bf16[2,1568,256...) while((s32[]{:T(128)}, bf16[2,1568,256]{1,2,0:T(8,128)(2,1)}, ...), condition=%wide.region_7.8_spmd, body=%wide.region_2.7_spmd.sunk | while | flops 1303268352 | bytes 87527496 | solution.py:166
  180.3 30.0 %while.57 = (s32[]{:T(128)}, bf16[2,784,4,64]{1,3,2,0:T(8,128)(2,1)}, f32[2,4,784,1]{2,1,3,0:T(4,128)S(1)}, bf16[2,784,4,64]{1,3,2,0:T(8,128)(2,1)}, bf16[1568,4...) while((s32[]{:T(128)}, bf16[2,784,4,64]{1,3,2,0:T(8,128)(2,1)}, ...), condition=%wide.region_6.6_spmd, body=%wide.region_3.5_spmd.sunk | while | flops 1303268352 | bytes 61734240 | solution.py:48
  220.9 30.0 %while.57 = (s32[]{:T(128)}, bf16[2,784,4,64]{1,3,2,0:T(8,128)(2,1)}, f32[2,4,784,1]{2,1,3,0:T(4,128)S(1)}, bf16[2,784,4,64]{1,3,2,0:T(8,128)(2,1)}, bf16[1568,4...) while((s32[]{:T(128)}, bf16[2,784,4,64]{1,3,2,0:T(8,128)(2,1)}, ...), condition=%wide.region_6.6_spmd, body=%wide.region_3.5_spmd.sunk | while | flops 1303268352 | bytes 61734240 | solution.py:48
  259.2 13.9 copy.84
  279.3 110.5 %reduce-scatter.25.cloned.1.call-done = bf16[392,2048]{1,0:T(8,128)(2,1)} async-done(((bf16[1568,2048]{1,0:T(8,128)(2,1)}), bf16[392,2048]{1,0:T(8,128)(2,1)}) %reduce-scatter.25.cloned.1.call-update) | async-done | bytes 1605648
  403.3 11.0 all-gather.14.cloned.1.call-done
  414.4 119.5 %all-gather.12.cloned.1.call-done = bf16[2,1568,1024]{2,1,0:T(8,128)(2,1)} async-done(((bf16[2,392,1024]{2,1,0:T(8,128)(2,1)}), bf16[2,1568,1024]{2,1,0:T(8,128)(2,1)}) %all-gather.12.cloned.1.call-update) | async-done | bytes 6422544 | tf_op jit(solution)/shard_map/all_gather | solution.py:186
  533.9 19.7 %fusion.109 = (u8[1568,1024]{1,0:T(8,128)(4,1)}, u8[1568,1024]{1,0:T(8,128)(4,1)}, f32[2,1568,1024]{2,1,0:T(8,128)}) fusion(f32[1024]{0:T(1024)S(1)} %convert_element_type.188, bf16[2,1568,1024]{2,1,0:T(8,128)(2,1)} %all-gather.12.cloned.1.call-done, bf16[1024,1024]{1,0:T(8,128)(2,1)} %all-gather.14.cloned.1.call-done), kind=kOutput, calls=%fused_computation.148 | convolution fusion | flops 6618415104 | bytes 24580096 | tf_op jit(solution)/shard_map/njz,zc->njc/dot_general | solution.py:187
  556.4 119.1 %all-gather.18.cloned.1.call-done = bf16[2,1568,1024]{2,1,0:T(8,128)(2,1)} async-done(((bf16[2,392,1024]{2,1,0:T(8,128)(2,1)}), bf16[2,1568,1024]{2,1,0:T(8,128)(2,1)}) %all-gather.18.cloned.1.call-update) | async-done | bytes 6422544 | tf_op jit(solution)/shard_map/all_gather | solution.py:202
  675.5 15.1 convert_reduce_fusion
  690.6 7.5 convolution_convert_fusion
  698.1 13.7 copy.88
  717.3 111.1 %reduce-scatter.29.cloned.1.call-done = bf16[392,2048]{1,0:T(8,128)(2,1)} async-done(((bf16[1568,2048]{1,0:T(8,128)(2,1)}), bf16[392,2048]{1,0:T(8,128)(2,1)}) %reduce-scatter.29.cloned.1.call-update) | async-done | bytes 1605648
  841.8 12.7 bitcast_convert_fusion.2
  854.6 31.3 %fusion.62 = bf16[2,1568,1024]{2,1,0:T(8,128)(2,1)S(1)} fusion(f32[2,1568,1024]{2,1,0:T(8,128)} %get-tuple-element.432, f32[1024]{0:T(1024)S(1)} %convert_element_type.188, u8[1568,1024]{1,0:T(8,128)(4,1)S(1)} %copy-done.29, u8[1568,1024]{1,0:T(8,128)(4,1)S(1)} %copy-done.28), kind=kLoop, calls=%fused_computation.65 | loop fusion | flops 227999744 | bytes 22482944 | tf_op jit(solution)/shard_map/convert_element_type | solution.py:191
  888.6 10.5 bitcast_convert_fusion.1
  899.2 60.8 %all-gather.20.cloned.1.call-done = bf16[2,1568,1024]{2,1,0:T(8,128)(2,1)} async-done(((bf16[2,392,1024]{2,1,0:T(8,128)(2,1)}), bf16[2,1568,1024]{2,1,0:T(8,128)(2,1)}) %all-gather.20.cloned.1.call-update) | async-done | bytes 6422544 | tf_op jit(solution)/shard_map/all_gather | solution.py:231
  967.3 388.1 %while.56 = (s32[]{:T(128)}, bf16[2,1568,256]{1,2,0:T(8,128)(2,1)}, bf16[2,1568,256]{2,1,0:T(8,128)(2,1)}, bf16[2,1568,256]{1,2,0:T(8,128)(2,1)}, bf16[2,1568,25...) while((s32[]{:T(128)}, bf16[2,1568,256]{1,2,0:T(8,128)(2,1)}, ...), condition=%wide.region_19.20_spmd, body=%wide.region_15.19_spmd.sunk | while | flops 3213581312 | bytes 417577472 | solution.py:238
  977.7 174.2 %while.58 = (s32[]{:T(128)}, f32[1568,4,64]{0,2,1:T(8,128)}, f32[1568,4,64]{0,2,1:T(8,128)}, bf16[2,784,4,64]{1,3,2,0:T(8,128)(2,1)}, bf16[2,784,4,64]{1,3,2,0:T...) while((s32[]{:T(128)}, f32[1568,4,64]{0,2,1:T(8,128)}, ...), condition=%wide.region_18.18_spmd.clone, body=%wide.region_16.17_spmd.clone.sunk | while | flops 3212778496 | bytes 332231680 | solution.py:88
  990.5 11.9 fusion.176
  1002.5 31.2 %fusion.179 = bf16[2,784,4,64]{1,3,2,0:T(8,128)(2,1)} fusion(bf16[2,784,4,64]{1,3,2,0:T(8,128)(2,1)} %get-tuple-element.710, s32[]{:T(128)S(6)} %copy.167, bf16[1568,4,64]{0,2,1:T(8,128)(2,1)} %get-tuple-element.723, f32[4,784,1568]{2,1,0:T(8,128)} %copy-done, f32[4,784,1568]{2,1,0:T(8,128)} %fusion.176), kind=kOutput, calls=%fused_computation.34.clone.1 | convolution fusion | flops 654199424 | bytes 84803584 | tf_op jit(solution)/shard_map/while/body/eval_jaxpr/while/body/eval_jaxpr/hbl,lhe->bhe/dot_general | solution.py:73
  1033.7 30.1 %fusion.177 = f32[1568,4,64]{0,2,1:T(8,128)S(1)} fusion(f32[4,784,1568]{2,1,0:T(8,128)} %copy-done, f32[4,784,1568]{2,1,0:T(8,128)} %fusion.176, f32[1568,4,64]{0,2,1:T(8,128)S(1)} %copy-done.13, pred[]{:T(512)S(6)} %compare.3, bf16[2,784,4,64]{1,3,2,0:T(8,128)(2,1)S(1)} %copy-done.2, s32[]{:T(128)S(6)} %copy.167), kind=kOutput, calls=%fused_computation.30.clone.1 | convolution fusion | flops 654801536 | bytes 87261192 | tf_op jit(solution)/shard_map/while/body/eval_jaxpr/while/body/eval_jaxpr/hbl,bhe->lhe/dot_general | solution.py:76
  1070.1 7.2 fusion.178
  1078.3 11.2 fusion.176
  1089.4 31.2 %fusion.179 = bf16[2,784,4,64]{1,3,2,0:T(8,128)(2,1)} fusion(bf16[2,784,4,64]{1,3,2,0:T(8,128)(2,1)} %get-tuple-element.710, s32[]{:T(128)S(6)} %copy.167, bf16[1568,4,64]{0,2,1:T(8,128)(2,1)} %get-tuple-element.723, f32[4,784,1568]{2,1,0:T(8,128)} %copy-done, f32[4,784,1568]{2,1,0:T(8,128)} %fusion.176), kind=kOutput, calls=%fused_computation.34.clone.1 | convolution fusion | flops 654199424 | bytes 84803584 | tf_op jit(solution)/shard_map/while/body/eval_jaxpr/while/body/eval_jaxpr/hbl,lhe->bhe/dot_general | solution.py:73
  1120.6 30.1 %fusion.177 = f32[1568,4,64]{0,2,1:T(8,128)S(1)} fusion(f32[4,784,1568]{2,1,0:T(8,128)} %copy-done, f32[4,784,1568]{2,1,0:T(8,128)} %fusion.176, f32[1568,4,64]{0,2,1:T(8,128)S(1)} %copy-done.13, pred[]{:T(512)S(6)} %compare.3, bf16[2,784,4,64]{1,3,2,0:T(8,128)(2,1)S(1)} %copy-done.2, s32[]{:T(128)S(6)} %copy.167), kind=kOutput, calls=%fused_computation.30.clone.1 | convolution fusion | flops 654801536 | bytes 87261192 | tf_op jit(solution)/shard_map/while/body/eval_jaxpr/while/body/eval_jaxpr/hbl,bhe->lhe/dot_general | solution.py:76
  1171.9 173.4 %while.58 = (s32[]{:T(128)}, f32[1568,4,64]{0,2,1:T(8,128)}, f32[1568,4,64]{0,2,1:T(8,128)}, bf16[2,784,4,64]{1,3,2,0:T(8,128)(2,1)}, bf16[2,784,4,64]{1,3,2,0:T...) while((s32[]{:T(128)}, f32[1568,4,64]{0,2,1:T(8,128)}, ...), condition=%wide.region_18.18_spmd.clone, body=%wide.region_16.17_spmd.clone.sunk | while | flops 3212778496 | bytes 332231680 | solution.py:88
  1184.6 11.2 fusion.176
  1195.8 31.2 %fusion.179 = bf16[2,784,4,64]{1,3,2,0:T(8,128)(2,1)} fusion(bf16[2,784,4,64]{1,3,2,0:T(8,128)(2,1)} %get-tuple-element.710, s32[]{:T(128)S(6)} %copy.167, bf16[1568,4,64]{0,2,1:T(8,128)(2,1)} %get-tuple-element.723, f32[4,784,1568]{2,1,0:T(8,128)} %copy-done, f32[4,784,1568]{2,1,0:T(8,128)} %fusion.176), kind=kOutput, calls=%fused_computation.34.clone.1 | convolution fusion | flops 654199424 | bytes 84803584 | tf_op jit(solution)/shard_map/while/body/eval_jaxpr/while/body/eval_jaxpr/hbl,lhe->bhe/dot_general | solution.py:73
  1227.0 30.1 %fusion.177 = f32[1568,4,64]{0,2,1:T(8,128)S(1)} fusion(f32[4,784,1568]{2,1,0:T(8,128)} %copy-done, f32[4,784,1568]{2,1,0:T(8,128)} %fusion.176, f32[1568,4,64]{0,2,1:T(8,128)S(1)} %copy-done.13, pred[]{:T(512)S(6)} %compare.3, bf16[2,784,4,64]{1,3,2,0:T(8,128)(2,1)S(1)} %copy-done.2, s32[]{:T(128)S(6)} %copy.167), kind=kOutput, calls=%fused_computation.30.clone.1 | convolution fusion | flops 654801536 | bytes 87261192 | tf_op jit(solution)/shard_map/while/body/eval_jaxpr/while/body/eval_jaxpr/hbl,bhe->lhe/dot_general | solution.py:76
  1263.4 7.2 fusion.178
  1271.6 11.2 fusion.176
  1282.8 31.2 %fusion.179 = bf16[2,784,4,64]{1,3,2,0:T(8,128)(2,1)} fusion(bf16[2,784,4,64]{1,3,2,0:T(8,128)(2,1)} %get-tuple-element.710, s32[]{:T(128)S(6)} %copy.167, bf16[1568,4,64]{0,2,1:T(8,128)(2,1)} %get-tuple-element.723, f32[4,784,1568]{2,1,0:T(8,128)} %copy-done, f32[4,784,1568]{2,1,0:T(8,128)} %fusion.176), kind=kOutput, calls=%fused_computation.34.clone.1 | convolution fusion | flops 654199424 | bytes 84803584 | tf_op jit(solution)/shard_map/while/body/eval_jaxpr/while/body/eval_jaxpr/hbl,lhe->bhe/dot_general | solution.py:73
  1314.0 30.1 %fusion.177 = f32[1568,4,64]{0,2,1:T(8,128)S(1)} fusion(f32[4,784,1568]{2,1,0:T(8,128)} %copy-done, f32[4,784,1568]{2,1,0:T(8,128)} %fusion.176, f32[1568,4,64]{0,2,1:T(8,128)S(1)} %copy-done.13, pred[]{:T(512)S(6)} %compare.3, bf16[2,784,4,64]{1,3,2,0:T(8,128)(2,1)S(1)} %copy-done.2, s32[]{:T(128)S(6)} %copy.167), kind=kOutput, calls=%fused_computation.30.clone.1 | convolution fusion | flops 654801536 | bytes 87261192 | tf_op jit(solution)/shard_map/while/body/eval_jaxpr/while/body/eval_jaxpr/hbl,bhe->lhe/dot_general | solution.py:76
  1367.0 10.2 fusion.119
  1377.2 10.2 convolution_convert_fusion.1
  1387.5 13.7 copy.86
  1406.8 11.1 reduce-scatter.17.cloned.1.call-done
  1417.9 7.6 bitcast_convert_fusion
  1425.5 13.7 copy.90
  1445.6 87.3 %reduce-scatter.27.cloned.1.call-done = bf16[392,2048]{1,0:T(8,128)(2,1)} async-done(((bf16[1568,2048]{1,0:T(8,128)(2,1)}), bf16[392,2048]{1,0:T(8,128)(2,1)}) %reduce-scatter.27.cloned.1.call-update) | async-done | bytes 1605648
  1539.4 48.4 %all-reduce.4.cloned.1.call-done = (bf16[3,256,256]{1,2,0:T(8,128)(2,1)}, bf16[256,256]{1,0:T(8,128)(2,1)}, bf16[256,1024]{1,0:T(8,128)(2,1)}, bf16[1024,256]{1,0:T(8,128)(2,1)}) async-done(((bf16[3,256,256]{1,2,0:T(8,128)(2,1)}, bf16[256,256]{1,0:T(8,128)(2,1)}, bf16[256,1024]{1,0:T(8,128)(2,1)}, bf16[1024,256]{1,0:T(8,128)(2,1)}), (bf16[3,256,256]{1,2,0:T(8,128)(2,1)}, bf16[256,256]{1,0:T(8,128)(2,1)}, ...) | async-done | bytes 1572880 | tf_op jit(solution)/shard_map/psum | solution.py:280
  1594.9 108.1 %reduce-scatter.31.cloned.1.call-done = bf16[392,2048]{1,0:T(8,128)(2,1)} async-done(((bf16[1568,2048]{1,0:T(8,128)(2,1)}), bf16[392,2048]{1,0:T(8,128)(2,1)}) %reduce-scatter.31.cloned.1.call-update) | async-done | bytes 1605648
  1711.6 41.9 %all-reduce = (f32[1024]{0:T(1024)S(1)}, f32[1024]{0:T(1024)S(1)}, f32[1024]{0:T(1024)S(1)}, f32[1024]{0:T(1024)S(1)}, f32[1024]{0:T(1024)S(1)}, /*index=5*/f32[...) all-reduce(f32[1024]{0:T(1024)S(1)} %get-tuple-element.338, ...), channel_id=1, replica_groups=mesh['tensor'=4,'group'=4,'cross'=2] {'tensor','group','cross'}, use_global_device_ids=true, to_apply=%region_24.25 | all-reduce | flops 12288 | bytes 98304 | tf_op jit(solution)/shard_map/psum | solution.py:285
  1759.1 7.1 fusion.97
  (373 shorter events, 296.2 us)
Async XLA Ops:
  7.2 26.3 %all-gather.10.cloned.1.call-start = ((), (), s32[]{:S(2)}) async-start(), calls=%async_computation.9 | async-start | bytes 1966080 | tf_op jit(solution)/shard_map/all_gather | solution.py:145
  7.9 146.1 %all-gather.8.cloned.1.call-start = ((), (), s32[]{:S(2)}) async-start(), calls=%async_computation.8 | async-start | bytes 8028160 | tf_op jit(solution)/shard_map/all_gather | solution.py:155
  15.6 374.2 %reduce-scatter.25.cloned.1.call-start = ((), (), s32[]{:S(2)}) async-start(), calls=%async_computation.19 | async-start | bytes 8028160
  278.6 115.7 %copy-start.4 = (bf16[2,392,1024]{2,1,0:T(8,128)(2,1)S(1)}, bf16[2,392,1024]{2,1,0:T(8,128)(2,1)}, u32[]{:S(2)}) copy-start(bf16[2,392,1024]{2,1,0:T(8,128)(2,1)} %param.24) | copy-start | bytes 4816900
  278.6 135.8 %all-gather.14.cloned.1.call-start = ((), (), s32[]{:S(2)}) async-start(), calls=%async_computation.11 | async-start | bytes 2621440 | tf_op jit(solution)/shard_map/all_gather | solution.py:147
  279.2 254.7 %all-gather.12.cloned.1.call-start = ((), (), s32[]{:S(2)}) async-start(), calls=%async_computation.10 | async-start | bytes 8028160 | tf_op jit(solution)/shard_map/all_gather | solution.py:186
  279.3 558.7 %copy-start.32 = (f32[1024]{0:T(1024)}, f32[1024]{0:T(1024)S(1)}, u32[]{:S(2)}) copy-start(f32[1024]{0:T(1024)S(1)} %convert_element_type.184) | copy-start | bytes 12292
  279.3 558.7 %copy-start.39 = (f32[1024]{0:T(1024)}, f32[1024]{0:T(1024)S(1)}, u32[]{:S(2)}) copy-start(f32[1024]{0:T(1024)S(1)} %convert_element_type.185) | copy-start | bytes 12292
  394.3 443.7 %copy-start.6 = (bf16[392,2,1024]{2,1,0:T(2,128)(2,1)}, bf16[392,2,1024]{2,1,0:T(2,128)(2,1)S(1)}, u32[]{:S(2)}) copy-start(bf16[392,2,1024]{2,1,0:T(2,128)(2,1)S(1)} %reshape.174) | copy-start | bytes 4816900
  394.9 443.1 %copy-start.34 = (f32[2,392]{1,0:T(2,128)}, f32[2,392]{1,0:T(2,128)S(1)}, u32[]{:S(2)}) copy-start(f32[2,392]{1,0:T(2,128)S(1)} %broadcast_multiply_fusion.4) | copy-start | bytes 9412
  395.8 442.2 %copy-start.41 = (f32[2,392]{1,0:T(2,128)}, f32[2,392]{1,0:T(2,128)S(1)}, u32[]{:S(2)}) copy-start(f32[2,392]{1,0:T(2,128)S(1)} %add_rsqrt_fusion) | copy-start | bytes 9412
  397.9 158.5 %all-gather.16.cloned.1.call-start = ((), (), s32[]{:S(2)}) async-start(), calls=%async_computation.12 | async-start | bytes 2621440 | tf_op jit(solution)/shard_map/all_gather | solution.py:148
  398.5 277.0 %all-gather.18.cloned.1.call-start = ((), (), s32[]{:S(2)}) async-start(), calls=%async_computation.13 | async-start | bytes 8028160 | tf_op jit(solution)/shard_map/all_gather | solution.py:202
  399.2 438.9 %copy-start.55 = (f32[2]{0:T(128)}, f32[2]{0:T(128)S(1)}, u32[]{:S(2)}) copy-start(f32[2]{0:T(128)S(1)} %compare_convert_fusion) | copy-start | bytes 28
  403.3 425.2 %reduce-scatter.29.cloned.1.call-start = ((), (), s32[]{:S(2)}) async-start(), calls=%async_computation.21 | async-start | bytes 8028160
  717.3 242.6 %all-gather.20.cloned.1.call-start = ((), (), s32[]{:S(2)}) async-start(), calls=%async_computation.14 | async-start | bytes 8028160 | tf_op jit(solution)/shard_map/all_gather | solution.py:231
  841.7 565.0 %reduce-scatter.21.cloned.1.call-start = ((), (), s32[]{:S(2)}) async-start(), calls=%async_computation.17 | async-start | bytes 2621440 | tf_op jit(solution)/shard_map/reduce_scatter | solution.py:272
  854.5 552.2 %reduce-scatter.23.cloned.1.call-start = ((), (), s32[]{:S(2)}) async-start(), calls=%async_computation.18 | async-start | bytes 2621440 | tf_op jit(solution)/shard_map/reduce_scatter | solution.py:275
  888.5 71.4 %copy-start.27 = (bf16[256,1024]{1,0:T(8,128)(2,1)S(1)}, bf16[256,1024]{1,0:T(8,128)(2,1)}, u32[]{:S(2)}) copy-start(bf16[256,1024]{1,0:T(8,128)(2,1)} %all_gather.26) | copy-start | bytes 1572868
  899.1 507.6 %reduce-scatter.19.cloned.1.call-start = ((), (), s32[]{:S(2)}) async-start(), calls=%async_computation.16 | async-start | bytes 655360 | tf_op jit(solution)/shard_map/reduce_scatter | solution.py:269
  1002.4 31.2 %copy-start.2 = (bf16[2,784,4,64]{1,3,2,0:T(8,128)(2,1)S(1)}, bf16[2,784,4,64]{1,3,2,0:T(8,128)(2,1)}, u32[]{:S(2)}) copy-start(bf16[2,784,4,64]{1,3,2,0:T(8,128)(2,1)} %get-tuple-element.722) | copy-start | bytes 2408452 | tf_op jit(solution)/shard_map/while/body/eval_jaxpr/while
  1002.5 31.2 %copy-start.13 = (f32[1568,4,64]{0,2,1:T(8,128)S(1)}, f32[1568,4,64]{0,2,1:T(8,128)}, u32[]{:S(2)}) copy-start(f32[1568,4,64]{0,2,1:T(8,128)} %get-tuple-element.708) | copy-start | bytes 4816900 | tf_op jit(solution)/shard_map/while/body/eval_jaxpr/while
  1089.4 31.2 %copy-start.2 = (bf16[2,784,4,64]{1,3,2,0:T(8,128)(2,1)S(1)}, bf16[2,784,4,64]{1,3,2,0:T(8,128)(2,1)}, u32[]{:S(2)}) copy-start(bf16[2,784,4,64]{1,3,2,0:T(8,128)(2,1)} %get-tuple-element.722) | copy-start | bytes 2408452 | tf_op jit(solution)/shard_map/while/body/eval_jaxpr/while
  1089.4 31.2 %copy-start.13 = (f32[1568,4,64]{0,2,1:T(8,128)S(1)}, f32[1568,4,64]{0,2,1:T(8,128)}, u32[]{:S(2)}) copy-start(f32[1568,4,64]{0,2,1:T(8,128)} %get-tuple-element.708) | copy-start | bytes 4816900 | tf_op jit(solution)/shard_map/while/body/eval_jaxpr/while
  1195.8 31.2 %copy-start.2 = (bf16[2,784,4,64]{1,3,2,0:T(8,128)(2,1)S(1)}, bf16[2,784,4,64]{1,3,2,0:T(8,128)(2,1)}, u32[]{:S(2)}) copy-start(bf16[2,784,4,64]{1,3,2,0:T(8,128)(2,1)} %get-tuple-element.722) | copy-start | bytes 2408452 | tf_op jit(solution)/shard_map/while/body/eval_jaxpr/while
  1195.8 31.2 %copy-start.13 = (f32[1568,4,64]{0,2,1:T(8,128)S(1)}, f32[1568,4,64]{0,2,1:T(8,128)}, u32[]{:S(2)}) copy-start(f32[1568,4,64]{0,2,1:T(8,128)} %get-tuple-element.708) | copy-start | bytes 4816900 | tf_op jit(solution)/shard_map/while/body/eval_jaxpr/while
  1282.8 31.2 %copy-start.13 = (f32[1568,4,64]{0,2,1:T(8,128)S(1)}, f32[1568,4,64]{0,2,1:T(8,128)}, u32[]{:S(2)}) copy-start(f32[1568,4,64]{0,2,1:T(8,128)} %get-tuple-element.708) | copy-start | bytes 4816900 | tf_op jit(solution)/shard_map/while/body/eval_jaxpr/while
  1366.9 50.9 %reduce-scatter.17.cloned.1.call-start = ((), (), s32[]{:S(2)}) async-start(), calls=%async_computation.15 | async-start | bytes 1966080 | tf_op jit(solution)/shard_map/reduce_scatter | solution.py:266
  1377.2 155.7 %reduce-scatter.27.cloned.1.call-start = ((), (), s32[]{:S(2)}) async-start(), calls=%async_computation.20 | async-start | bytes 8028160
  1406.6 181.2 %all-reduce.4.cloned.1.call-start = ((), (), s32[]{:S(2)}) async-start(), calls=%async_computation.23 | async-start | bytes 3145728 | tf_op jit(solution)/shard_map/psum | solution.py:280
  1417.9 285.2 %reduce-scatter.31.cloned.1.call-start = ((), (), s32[]{:S(2)}) async-start(), calls=%async_computation.22 | async-start | bytes 8028160
  1444.7 93.6 %copy-start.18 = (bf16[2,1568,256]{1,2,0:T(8,128)(2,1)S(1)}, bf16[2,1568,256]{1,2,0:T(8,128)(2,1)}, u32[]{:S(2)}) copy-start(bf16[2,1568,256]{1,2,0:T(8,128)(2,1)} %get-tuple-element.183) | copy-start | bytes 4816900
  1591.5 116.8 %copy-start.5 = (bf16[2,392,1024]{2,1,0:T(8,128)(2,1)S(1)}, bf16[2,392,1024]{2,1,0:T(8,128)(2,1)}, u32[]{:S(2)}) copy-start(bf16[2,392,1024]{2,1,0:T(8,128)(2,1)} %param.24) | copy-start | bytes 4816900
  1591.5 116.8 %copy-start.38 = (f32[2,392]{1,0:T(2,128)S(1)}, f32[2,392]{1,0:T(2,128)}, u32[]{:S(2)}) copy-start(f32[2,392]{1,0:T(2,128)} %copy-done.37) | copy-start | bytes 9412
  1591.5 116.8 %copy-start.44 = (f32[1024]{0:T(1024)S(1)}, f32[1024]{0:T(1024)}, u32[]{:S(2)}) copy-start(f32[1024]{0:T(1024)} %copy-done.43) | copy-start | bytes 12292
  1591.5 116.8 %copy-start.46 = (f32[2,392]{1,0:T(2,128)S(1)}, f32[2,392]{1,0:T(2,128)}, u32[]{:S(2)}) copy-start(f32[2,392]{1,0:T(2,128)} %copy-done.45) | copy-start | bytes 9412
  1594.8 116.7 %copy-start.51 = (f32[1024]{0:T(1024)S(1)}, f32[1024]{0:T(1024)}, u32[]{:S(2)}) copy-start(f32[1024]{0:T(1024)} %get-tuple-element.417) | copy-start | bytes 12292
  1594.8 116.7 %copy-start.52 = (f32[1024]{0:T(1024)S(1)}, f32[1024]{0:T(1024)}, u32[]{:S(2)}) copy-start(f32[1024]{0:T(1024)} %get-tuple-element.336) | copy-start | bytes 12292
  1594.8 116.7 %copy-start.53 = (f32[1024]{0:T(1024)S(1)}, f32[1024]{0:T(1024)}, u32[]{:S(2)}) copy-start(f32[1024]{0:T(1024)} %get-tuple-element.342) | copy-start | bytes 12292
  1594.8 116.7 %copy-start.54 = (f32[1024]{0:T(1024)S(1)}, f32[1024]{0:T(1024)}, u32[]{:S(2)}) copy-start(f32[1024]{0:T(1024)} %get-tuple-element.419) | copy-start | bytes 12292
  1594.9 164.2 %copy-start.7 = (bf16[392,2,1024]{2,1,0:T(2,128)(2,1)S(1)}, bf16[392,2,1024]{2,1,0:T(2,128)(2,1)}, u32[]{:S(2)}) copy-start(bf16[392,2,1024]{2,1,0:T(2,128)(2,1)} %copy-done.6) | copy-start | bytes 4816900
  1594.9 164.2 %copy-start.33 = (f32[1024]{0:T(1024)S(1)}, f32[1024]{0:T(1024)}, u32[]{:S(2)}) copy-start(f32[1024]{0:T(1024)} %copy-done.32) | copy-start | bytes 12292
  1594.9 164.2 %copy-start.35 = (f32[2,392]{1,0:T(2,128)S(1)}, f32[2,392]{1,0:T(2,128)}, u32[]{:S(2)}) copy-start(f32[2,392]{1,0:T(2,128)} %copy-done.34) | copy-start | bytes 9412
  1594.9 164.2 %copy-start.40 = (f32[1024]{0:T(1024)S(1)}, f32[1024]{0:T(1024)}, u32[]{:S(2)}) copy-start(f32[1024]{0:T(1024)} %copy-done.39) | copy-start | bytes 12292
  1594.9 164.2 %copy-start.42 = (f32[2,392]{1,0:T(2,128)S(1)}, f32[2,392]{1,0:T(2,128)}, u32[]{:S(2)}) copy-start(f32[2,392]{1,0:T(2,128)} %copy-done.41) | copy-start | bytes 9412
  1594.9 164.2 %copy-start.48 = (f32[2,392]{1,0:T(2,128)S(1)}, f32[2,392]{1,0:T(2,128)}, u32[]{:S(2)}) copy-start(f32[2,392]{1,0:T(2,128)} %copy-done.47) | copy-start | bytes 9412
  1594.9 164.2 %copy-start.50 = (f32[2,392]{1,0:T(2,128)S(1)}, f32[2,392]{1,0:T(2,128)}, u32[]{:S(2)}) copy-start(f32[2,392]{1,0:T(2,128)} %copy-done.49) | copy-start | bytes 9412
  1594.9 164.2 %copy-start.56 = (f32[2]{0:T(128)S(1)}, f32[2]{0:T(128)}, u32[]{:S(2)}) copy-start(f32[2]{0:T(128)} %copy-done.55) | copy-start | bytes 28
  (58 other events, 272.0 us)
Sparse Core Ops, SparseCore 0:
  9.6 23.8 all-gather.9
  35.6 118.3 all-gather.7
  278.7 111.0 reduce-scatter.24
  391.2 23.0 all-gather.13
  416.4 117.4 all-gather.11
  535.3 21.0 all-gather.15
  557.9 117.4 all-gather.17
  717.4 111.0 reduce-scatter.28
  841.8 118.0 all-gather.19
  962.3 29.5 reduce-scatter.20
  994.6 31.4 reduce-scatter.22
  1367.1 19.8 reduce-scatter.18
  1389.6 28.1 reduce-scatter.16
  1420.0 112.8 reduce-scatter.26
  1535.2 52.5 all-reduce.3
  1590.1 112.8 reduce-scatter.30
where the time goes:
time: 1780 us; the launch traced here: 1770 us
  waiting for transfers between devices  919 us (52%)
  matrix products  495 us (28%)
  local copies, waits for them, and re-layouts  199 us (11%)
  other arithmetic  89.5 us (5%)
  blocking collectives  52.7 us (3%)
    unnamed x20, waiting for transfers between devices  419 us
    dot_general x4, matrix products, one_part(): jnp.einsum('hbl,lhe->bhe', logit_grad, key_heads, preferred_element_type=...  125 us
    all_gather x1, waiting for transfers between devices, local(): first_gathered = lax.all_gather(first_rows, 'tensor', axis=1, tiled=True)  121 us
    dot_general x4, matrix products, one_part(): jnp.einsum('hbl,bhe->lhe', logit_grad, query_part, preferred_element_type...  120 us
    all_gather x1, waiting for transfers between devices, local(): second_gathered = lax.all_gather(second_rows, 'tensor', axis=1, tiled=True)  120 us
    all_gather x1, waiting for transfers between devices, local(): feed_grad_gathered = lax.all_gather(feed_grad, 'tensor', axis=1, tiled=True)  119 us
    unnamed x117, local copies, waits for them, and re-layouts  103 us
    all_gather x1, waiting for transfers between devices, local(): branch_gathered = lax.all_gather(branch_grad, 'tensor', axis=1, tiled=True)  60.8 us
  transfers between devices with their start and end apart: 16, of which 13 were waited for; matrix products, arithmetic and copies ran while one was open for 32% of the time, Pallas kernels for 0%

commit v1 on v0

--- a/solution.py
+++ b/solution.py
@@ -277,7 +277,9 @@
         ).astype(jnp.float32),
     )
     large_sums = (
-        lax.psum(group_parts[0].astype(jnp.bfloat16), "cross").astype(jnp.float32),
+        jnp.sum(lax.all_gather(group_parts[0].astype(jnp.bfloat16), "cross"), axis=0).astype(
+            jnp.float32
+        ),
         lax.psum(group_parts[1].astype(jnp.bfloat16), "cross").astype(jnp.float32),
         lax.psum(group_parts[2].astype(jnp.bfloat16), "cross").astype(jnp.float32),
         lax.psum(group_parts[3].astype(jnp.bfloat16), "cross").astype(jnp.float32),

time: 1780 us -> 1660 us (0.933)
  waiting for transfers between devices: 919 us -> 787 us
    unnamed x20, waiting for transfers between devices: 419 us -> 324 us
    psum x1, waiting for transfers between devices: 48.4 us -> 0.01 us  [local(): lax.psum(group_parts[1].astype(jnp.bfloat16), 'cross').astype(jnp.float32)]
    unnamed x117 -> x114, local copies, waits for them, and re-layouts: 103 us -> 104 us
  transfers between devices with their start and end apart: 16 -> 16, of which waited for: 13 -> 11; matrix products, arithmetic and copies ran while one was open for 32% -> 34% of each run, Pallas kernels for 0% -> 0%
where the time goes in v1:
time: 1660 us; the launch traced here: 1650 us
  waiting for transfers between devices  787 us (47%)
  matrix products  494 us (30%)
  local copies, waits for them, and re-layouts  201 us (12%)
  other arithmetic  90.7 us (5%)
  blocking collectives  64 us (4%)
    unnamed x20, waiting for transfers between devices  324 us
    dot_general x4, matrix products, one_part(): jnp.einsum('hbl,lhe->bhe', logit_grad, key_heads, preferred_element_type=...  125 us
    all_gather x1, waiting for transfers between devices, local(): first_gathered = lax.all_gather(first_rows, 'tensor', axis=1, tiled=True)  121 us
    dot_general x4, matrix products, one_part(): jnp.einsum('hbl,bhe->lhe', logit_grad, query_part, preferred_element_type...  120 us
    all_gather x1, waiting for transfers between devices, local(): second_gathered = lax.all_gather(second_rows, 'tensor', axis=1, tiled=True)  120 us
    all_gather x1, waiting for transfers between devices, local(): feed_grad_gathered = lax.all_gather(feed_grad, 'tensor', axis=1, tiled=True)  119 us
    unnamed x114, local copies, waits for them, and re-layouts  104 us
    all_gather x1, waiting for transfers between devices, local(): branch_gathered = lax.all_gather(branch_grad, 'tensor', axis=1, tiled=True)  60.7 us
  transfers between devices with their start and end apart: 16, of which 11 were waited for; matrix products, arithmetic and copies ran while one was open for 34% of the time, Pallas kernels for 0%

profile of v1, /device:TPU:0, one launch (start us, length us, event | category | flops | bytes accessed | tf_op | source)
XLA Modules:
  0.0 1654.8 jit_solution(4293863833872528642)
XLA Ops:
  15.8 10.8 all_gather.32
  26.7 6.8 all-gather.11.cloned.1.call-done
  33.5 120.5 %all-gather.9.cloned.1.call-done = bf16[2,1568,1024]{2,1,0:T(8,128)(2,1)} async-done(((bf16[2,392,1024]{2,1,0:T(8,128)(2,1)}), bf16[2,1568,1024]{2,1,0:T(8,128)(2,1)}) %all-gather.9.cloned.1.call-update) | async-done | bytes 6422544 | tf_op jit(solution)/shard_map/all_gather | solution.py:155
  154.0 7.8 fusion.79
  173.8 81.3 %while.54 = (s32[]{:T(128)}, bf16[2,1568,256]{1,2,0:T(8,128)(2,1)}, f32[2,2,4,784,1]{3,2,1,4,0:T(4,128)}, bf16[2,1568,256]{1,2,0:T(8,128)(2,1)}, bf16[2,1568,256...) while((s32[]{:T(128)}, bf16[2,1568,256]{1,2,0:T(8,128)(2,1)}, ...), condition=%wide.region_7.8_spmd, body=%wide.region_2.7_spmd.sunk | while | flops 1303268352 | bytes 87527496 | solution.py:166
  180.3 30.0 %while.57 = (s32[]{:T(128)}, bf16[2,784,4,64]{1,3,2,0:T(8,128)(2,1)}, f32[2,4,784,1]{2,1,3,0:T(4,128)S(1)}, bf16[2,784,4,64]{1,3,2,0:T(8,128)(2,1)}, bf16[1568,4...) while((s32[]{:T(128)}, bf16[2,784,4,64]{1,3,2,0:T(8,128)(2,1)}, ...), condition=%wide.region_6.6_spmd, body=%wide.region_3.5_spmd.sunk | while | flops 1303268352 | bytes 61734240 | solution.py:48
  220.8 30.0 %while.57 = (s32[]{:T(128)}, bf16[2,784,4,64]{1,3,2,0:T(8,128)(2,1)}, f32[2,4,784,1]{2,1,3,0:T(4,128)S(1)}, bf16[2,784,4,64]{1,3,2,0:T(8,128)(2,1)}, bf16[1568,4...) while((s32[]{:T(128)}, bf16[2,784,4,64]{1,3,2,0:T(8,128)(2,1)}, ...), condition=%wide.region_6.6_spmd, body=%wide.region_3.5_spmd.sunk | while | flops 1303268352 | bytes 61734240 | solution.py:48
  259.2 14.0 copy.84
  279.3 110.5 %reduce-scatter.25.cloned.1.call-done = bf16[392,2048]{1,0:T(8,128)(2,1)} async-done(((bf16[1568,2048]{1,0:T(8,128)(2,1)}), bf16[392,2048]{1,0:T(8,128)(2,1)}) %reduce-scatter.25.cloned.1.call-update) | async-done | bytes 1605648
  403.3 11.1 all-gather.15.cloned.1.call-done
  414.3 119.5 %all-gather.13.cloned.1.call-done = bf16[2,1568,1024]{2,1,0:T(8,128)(2,1)} async-done(((bf16[2,392,1024]{2,1,0:T(8,128)(2,1)}), bf16[2,1568,1024]{2,1,0:T(8,128)(2,1)}) %all-gather.13.cloned.1.call-update) | async-done | bytes 6422544 | tf_op jit(solution)/shard_map/all_gather | solution.py:186
  533.8 19.8 %fusion.109 = (u8[1568,1024]{1,0:T(8,128)(4,1)}, u8[1568,1024]{1,0:T(8,128)(4,1)}, f32[2,1568,1024]{2,1,0:T(8,128)}) fusion(f32[1024]{0:T(1024)S(1)} %convert_element_type.190, bf16[2,1568,1024]{2,1,0:T(8,128)(2,1)} %all-gather.13.cloned.1.call-done, bf16[1024,1024]{1,0:T(8,128)(2,1)} %all-gather.15.cloned.1.call-done), kind=kOutput, calls=%fused_computation.148 | convolution fusion | flops 6618415104 | bytes 24580096 | tf_op jit(solution)/shard_map/njz,zc->njc/dot_general | solution.py:187
  556.3 119.1 %all-gather.19.cloned.1.call-done = bf16[2,1568,1024]{2,1,0:T(8,128)(2,1)} async-done(((bf16[2,392,1024]{2,1,0:T(8,128)(2,1)}), bf16[2,1568,1024]{2,1,0:T(8,128)(2,1)}) %all-gather.19.cloned.1.call-update) | async-done | bytes 6422544 | tf_op jit(solution)/shard_map/all_gather | solution.py:202
  675.4 15.1 convert_reduce_fusion
  690.5 7.5 convolution_convert_fusion
  698.0 13.7 copy.88
  717.2 111.2 %reduce-scatter.29.cloned.1.call-done = bf16[392,2048]{1,0:T(8,128)(2,1)} async-done(((bf16[1568,2048]{1,0:T(8,128)(2,1)}), bf16[392,2048]{1,0:T(8,128)(2,1)}) %reduce-scatter.29.cloned.1.call-update) | async-done | bytes 1605648
  841.8 12.6 bitcast_convert_fusion.2
  854.5 31.3 %fusion.62 = bf16[2,1568,1024]{2,1,0:T(8,128)(2,1)S(1)} fusion(f32[2,1568,1024]{2,1,0:T(8,128)} %get-tuple-element.401, f32[1024]{0:T(1024)S(1)} %convert_element_type.190, u8[1568,1024]{1,0:T(8,128)(4,1)S(1)} %copy-done.29, u8[1568,1024]{1,0:T(8,128)(4,1)S(1)} %copy-done.28), kind=kLoop, calls=%fused_computation.65 | loop fusion | flops 227999744 | bytes 22482944 | tf_op jit(solution)/shard_map/convert_element_type | solution.py:191
  888.5 10.6 bitcast_convert_fusion.1
  899.2 60.7 %all-gather.21.cloned.1.call-done = bf16[2,1568,1024]{2,1,0:T(8,128)(2,1)} async-done(((bf16[2,392,1024]{2,1,0:T(8,128)(2,1)}), bf16[2,1568,1024]{2,1,0:T(8,128)(2,1)}) %all-gather.21.cloned.1.call-update) | async-done | bytes 6422544 | tf_op jit(solution)/shard_map/all_gather | solution.py:231
  965.5 11.2 convolution_convert_fusion.1
  976.7 13.7 copy.86
  1004.3 387.9 %while.56 = (s32[]{:T(128)}, bf16[2,1568,256]{1,2,0:T(8,128)(2,1)}, bf16[2,1568,256]{2,1,0:T(8,128)(2,1)}, bf16[2,1568,256]{1,2,0:T(8,128)(2,1)}, bf16[2,1568,25...) while((s32[]{:T(128)}, bf16[2,1568,256]{1,2,0:T(8,128)(2,1)}, ...), condition=%wide.region_19.20_spmd, body=%wide.region_15.19_spmd.sunk | while | flops 3213581312 | bytes 417577472 | solution.py:238
  1014.6 173.9 %while.58 = (s32[]{:T(128)}, f32[1568,4,64]{0,2,1:T(8,128)}, f32[1568,4,64]{0,2,1:T(8,128)}, bf16[2,784,4,64]{1,3,2,0:T(8,128)(2,1)}, bf16[2,784,4,64]{1,3,2,0:T...) while((s32[]{:T(128)}, f32[1568,4,64]{0,2,1:T(8,128)}, ...), condition=%wide.region_18.18_spmd.clone, body=%wide.region_16.17_spmd.clone.sunk | while | flops 3212778496 | bytes 332231680 | solution.py:88
  1027.4 11.4 fusion.176
  1038.8 31.2 %fusion.179 = bf16[2,784,4,64]{1,3,2,0:T(8,128)(2,1)} fusion(bf16[2,784,4,64]{1,3,2,0:T(8,128)(2,1)} %get-tuple-element.679, s32[]{:T(128)S(6)} %copy.169, bf16[1568,4,64]{0,2,1:T(8,128)(2,1)} %get-tuple-element.692, f32[4,784,1568]{2,1,0:T(8,128)} %copy-done, f32[4,784,1568]{2,1,0:T(8,128)} %fusion.176), kind=kOutput, calls=%fused_computation.34.clone.1 | convolution fusion | flops 654199424 | bytes 84803584 | tf_op jit(solution)/shard_map/while/body/eval_jaxpr/while/body/eval_jaxpr/hbl,lhe->bhe/dot_general | solution.py:73
  1070.0 30.1 %fusion.177 = f32[1568,4,64]{0,2,1:T(8,128)S(1)} fusion(f32[4,784,1568]{2,1,0:T(8,128)} %copy-done, f32[4,784,1568]{2,1,0:T(8,128)} %fusion.176, f32[1568,4,64]{0,2,1:T(8,128)S(1)} %copy-done.13, pred[]{:T(512)S(6)} %compare.3, bf16[2,784,4,64]{1,3,2,0:T(8,128)(2,1)S(1)} %copy-done.2, s32[]{:T(128)S(6)} %copy.169), kind=kOutput, calls=%fused_computation.30.clone.1 | convolution fusion | flops 654801536 | bytes 87261192 | tf_op jit(solution)/shard_map/while/body/eval_jaxpr/while/body/eval_jaxpr/hbl,bhe->lhe/dot_general | solution.py:76
  1106.4 7.1 fusion.178
  1114.8 11.2 fusion.176
  1126.0 31.2 %fusion.179 = bf16[2,784,4,64]{1,3,2,0:T(8,128)(2,1)} fusion(bf16[2,784,4,64]{1,3,2,0:T(8,128)(2,1)} %get-tuple-element.679, s32[]{:T(128)S(6)} %copy.169, bf16[1568,4,64]{0,2,1:T(8,128)(2,1)} %get-tuple-element.692, f32[4,784,1568]{2,1,0:T(8,128)} %copy-done, f32[4,784,1568]{2,1,0:T(8,128)} %fusion.176), kind=kOutput, calls=%fused_computation.34.clone.1 | convolution fusion | flops 654199424 | bytes 84803584 | tf_op jit(solution)/shard_map/while/body/eval_jaxpr/while/body/eval_jaxpr/hbl,lhe->bhe/dot_general | solution.py:73
  1157.2 30.1 %fusion.177 = f32[1568,4,64]{0,2,1:T(8,128)S(1)} fusion(f32[4,784,1568]{2,1,0:T(8,128)} %copy-done, f32[4,784,1568]{2,1,0:T(8,128)} %fusion.176, f32[1568,4,64]{0,2,1:T(8,128)S(1)} %copy-done.13, pred[]{:T(512)S(6)} %compare.3, bf16[2,784,4,64]{1,3,2,0:T(8,128)(2,1)S(1)} %copy-done.2, s32[]{:T(128)S(6)} %copy.169), kind=kOutput, calls=%fused_computation.30.clone.1 | convolution fusion | flops 654801536 | bytes 87261192 | tf_op jit(solution)/shard_map/while/body/eval_jaxpr/while/body/eval_jaxpr/hbl,bhe->lhe/dot_general | solution.py:76
  1208.7 173.3 %while.58 = (s32[]{:T(128)}, f32[1568,4,64]{0,2,1:T(8,128)}, f32[1568,4,64]{0,2,1:T(8,128)}, bf16[2,784,4,64]{1,3,2,0:T(8,128)(2,1)}, bf16[2,784,4,64]{1,3,2,0:T...) while((s32[]{:T(128)}, f32[1568,4,64]{0,2,1:T(8,128)}, ...), condition=%wide.region_18.18_spmd.clone, body=%wide.region_16.17_spmd.clone.sunk | while | flops 3212778496 | bytes 332231680 | solution.py:88
  1221.3 11.2 fusion.176
  1232.5 31.2 %fusion.179 = bf16[2,784,4,64]{1,3,2,0:T(8,128)(2,1)} fusion(bf16[2,784,4,64]{1,3,2,0:T(8,128)(2,1)} %get-tuple-element.679, s32[]{:T(128)S(6)} %copy.169, bf16[1568,4,64]{0,2,1:T(8,128)(2,1)} %get-tuple-element.692, f32[4,784,1568]{2,1,0:T(8,128)} %copy-done, f32[4,784,1568]{2,1,0:T(8,128)} %fusion.176), kind=kOutput, calls=%fused_computation.34.clone.1 | convolution fusion | flops 654199424 | bytes 84803584 | tf_op jit(solution)/shard_map/while/body/eval_jaxpr/while/body/eval_jaxpr/hbl,lhe->bhe/dot_general | solution.py:73
  1263.7 30.1 %fusion.177 = f32[1568,4,64]{0,2,1:T(8,128)S(1)} fusion(f32[4,784,1568]{2,1,0:T(8,128)} %copy-done, f32[4,784,1568]{2,1,0:T(8,128)} %fusion.176, f32[1568,4,64]{0,2,1:T(8,128)S(1)} %copy-done.13, pred[]{:T(512)S(6)} %compare.3, bf16[2,784,4,64]{1,3,2,0:T(8,128)(2,1)S(1)} %copy-done.2, s32[]{:T(128)S(6)} %copy.169), kind=kOutput, calls=%fused_computation.30.clone.1 | convolution fusion | flops 654801536 | bytes 87261192 | tf_op jit(solution)/shard_map/while/body/eval_jaxpr/while/body/eval_jaxpr/hbl,bhe->lhe/dot_general | solution.py:76
  1300.1 7.1 fusion.178
  1308.3 11.2 fusion.176
  1319.5 31.2 %fusion.179 = bf16[2,784,4,64]{1,3,2,0:T(8,128)(2,1)} fusion(bf16[2,784,4,64]{1,3,2,0:T(8,128)(2,1)} %get-tuple-element.679, s32[]{:T(128)S(6)} %copy.169, bf16[1568,4,64]{0,2,1:T(8,128)(2,1)} %get-tuple-element.692, f32[4,784,1568]{2,1,0:T(8,128)} %copy-done, f32[4,784,1568]{2,1,0:T(8,128)} %fusion.176), kind=kOutput, calls=%fused_computation.34.clone.1 | convolution fusion | flops 654199424 | bytes 84803584 | tf_op jit(solution)/shard_map/while/body/eval_jaxpr/while/body/eval_jaxpr/hbl,lhe->bhe/dot_general | solution.py:73
  1350.6 30.1 %fusion.177 = f32[1568,4,64]{0,2,1:T(8,128)S(1)} fusion(f32[4,784,1568]{2,1,0:T(8,128)} %copy-done, f32[4,784,1568]{2,1,0:T(8,128)} %fusion.176, f32[1568,4,64]{0,2,1:T(8,128)S(1)} %copy-done.13, pred[]{:T(512)S(6)} %compare.3, bf16[2,784,4,64]{1,3,2,0:T(8,128)(2,1)S(1)} %copy-done.2, s32[]{:T(128)S(6)} %copy.169), kind=kOutput, calls=%fused_computation.30.clone.1 | convolution fusion | flops 654801536 | bytes 87261192 | tf_op jit(solution)/shard_map/while/body/eval_jaxpr/while/body/eval_jaxpr/hbl,bhe->lhe/dot_general | solution.py:76
  1397.4 9.9 fusion.119
  1407.4 7.4 bitcast_convert_fusion
  1414.8 13.7 copy.90
  1447.2 22.3 %reduce-scatter.17.cloned.1.call-done = bf16[3,256,256]{1,2,0:T(8,128)(2,1)} async-done(((bf16[3,1024,256]{1,2,0:T(8,128)(2,1)}), bf16[3,256,256]{1,2,0:T(8,128)(2,1)}) %reduce-scatter.17.cloned.1.call-update) | async-done | bytes 393232 | tf_op jit(solution)/shard_map/reduce_scatter | solution.py:266
  1470.7 11.5 all-gather
  1483.9 100.8 %reduce-scatter.31.cloned.1.call-done = bf16[392,2048]{1,0:T(8,128)(2,1)} async-done(((bf16[1568,2048]{1,0:T(8,128)(2,1)}), bf16[392,2048]{1,0:T(8,128)(2,1)}) %reduce-scatter.31.cloned.1.call-update) | async-done | bytes 1605648
  1593.5 41.6 %all-reduce = (f32[1024]{0:T(1024)S(1)}, f32[1024]{0:T(1024)S(1)}, f32[1024]{0:T(1024)S(1)}, f32[1024]{0:T(1024)S(1)}, f32[1024]{0:T(1024)S(1)}, /*index=5*/f32[...) all-reduce(f32[1024]{0:T(1024)S(1)} %get-tuple-element.308, ...), channel_id=1, replica_groups=mesh['tensor'=4,'group'=4,'cross'=2] {'tensor','group','cross'}, use_global_device_ids=true, to_apply=%region_24.25 | all-reduce | flops 12288 | bytes 98304 | tf_op jit(solution)/shard_map/psum | solution.py:287
  1640.8 7.1 fusion.97
  (373 shorter events, 291.9 us)
Async XLA Ops:
  7.2 26.3 %all-gather.11.cloned.1.call-start = ((), (), s32[]{:S(2)}) async-start(), calls=%async_computation.9 | async-start | bytes 1966080 | tf_op jit(solution)/shard_map/all_gather | solution.py:145
  7.9 146.1 %all-gather.9.cloned.1.call-start = ((), (), s32[]{:S(2)}) async-start(), calls=%async_computation.8 | async-start | bytes 8028160 | tf_op jit(solution)/shard_map/all_gather | solution.py:155
  15.6 374.2 %reduce-scatter.25.cloned.1.call-start = ((), (), s32[]{:S(2)}) async-start(), calls=%async_computation.19 | async-start | bytes 8028160
  278.5 115.7 %copy-start.4 = (bf16[2,392,1024]{2,1,0:T(8,128)(2,1)S(1)}, bf16[2,392,1024]{2,1,0:T(8,128)(2,1)}, u32[]{:S(2)}) copy-start(bf16[2,392,1024]{2,1,0:T(8,128)(2,1)} %param.24) | copy-start | bytes 4816900
  278.6 135.8 %all-gather.15.cloned.1.call-start = ((), (), s32[]{:S(2)}) async-start(), calls=%async_computation.11 | async-start | bytes 2621440 | tf_op jit(solution)/shard_map/all_gather | solution.py:147
  279.1 254.7 %all-gather.13.cloned.1.call-start = ((), (), s32[]{:S(2)}) async-start(), calls=%async_computation.10 | async-start | bytes 8028160 | tf_op jit(solution)/shard_map/all_gather | solution.py:186
  279.2 558.7 %copy-start.30 = (f32[1024]{0:T(1024)}, f32[1024]{0:T(1024)S(1)}, u32[]{:S(2)}) copy-start(f32[1024]{0:T(1024)S(1)} %convert_element_type.186) | copy-start | bytes 12292
  279.2 558.7 %copy-start.37 = (f32[1024]{0:T(1024)}, f32[1024]{0:T(1024)S(1)}, u32[]{:S(2)}) copy-start(f32[1024]{0:T(1024)S(1)} %convert_element_type.187) | copy-start | bytes 12292
  394.3 443.7 %copy-start.6 = (bf16[392,2,1024]{2,1,0:T(2,128)(2,1)}, bf16[392,2,1024]{2,1,0:T(2,128)(2,1)S(1)}, u32[]{:S(2)}) copy-start(bf16[392,2,1024]{2,1,0:T(2,128)(2,1)S(1)} %reshape.175) | copy-start | bytes 4816900
  394.9 443.1 %copy-start.32 = (f32[2,392]{1,0:T(2,128)}, f32[2,392]{1,0:T(2,128)S(1)}, u32[]{:S(2)}) copy-start(f32[2,392]{1,0:T(2,128)S(1)} %broadcast_multiply_fusion.4) | copy-start | bytes 9412
  395.8 442.2 %copy-start.39 = (f32[2,392]{1,0:T(2,128)}, f32[2,392]{1,0:T(2,128)S(1)}, u32[]{:S(2)}) copy-start(f32[2,392]{1,0:T(2,128)S(1)} %add_rsqrt_fusion) | copy-start | bytes 9412
  397.8 158.5 %all-gather.17.cloned.1.call-start = ((), (), s32[]{:S(2)}) async-start(), calls=%async_computation.12 | async-start | bytes 2621440 | tf_op jit(solution)/shard_map/all_gather | solution.py:148
  398.4 277.0 %all-gather.19.cloned.1.call-start = ((), (), s32[]{:S(2)}) async-start(), calls=%async_computation.13 | async-start | bytes 8028160 | tf_op jit(solution)/shard_map/all_gather | solution.py:202
  399.1 438.9 %copy-start.53 = (f32[2]{0:T(128)}, f32[2]{0:T(128)S(1)}, u32[]{:S(2)}) copy-start(f32[2]{0:T(128)S(1)} %compare_convert_fusion) | copy-start | bytes 28
  403.2 425.2 %reduce-scatter.29.cloned.1.call-start = ((), (), s32[]{:S(2)}) async-start(), calls=%async_computation.21 | async-start | bytes 8028160
  717.2 242.7 %all-gather.21.cloned.1.call-start = ((), (), s32[]{:S(2)}) async-start(), calls=%async_computation.14 | async-start | bytes 8028160 | tf_op jit(solution)/shard_map/all_gather | solution.py:231
  841.8 555.5 %reduce-scatter.21.cloned.1.call-start = ((), (), s32[]{:S(2)}) async-start(), calls=%async_computation.17 | async-start | bytes 2621440 | tf_op jit(solution)/shard_map/reduce_scatter | solution.py:272
  854.5 542.8 %reduce-scatter.23.cloned.1.call-start = ((), (), s32[]{:S(2)}) async-start(), calls=%async_computation.18 | async-start | bytes 2621440 | tf_op jit(solution)/shard_map/reduce_scatter | solution.py:275
  888.5 71.4 %copy-start.25 = (bf16[2,1568,256]{1,2,0:T(8,128)(2,1)S(1)}, bf16[2,1568,256]{1,2,0:T(8,128)(2,1)}, u32[]{:S(2)}) copy-start(bf16[2,1568,256]{1,2,0:T(8,128)(2,1)} %get-tuple-element.179) | copy-start | bytes 4816900
  899.1 498.1 %reduce-scatter.19.cloned.1.call-start = ((), (), s32[]{:S(2)}) async-start(), calls=%async_computation.16 | async-start | bytes 655360 | tf_op jit(solution)/shard_map/reduce_scatter | solution.py:269
  965.5 469.4 %reduce-scatter.27.cloned.1.call-start = ((), (), s32[]{:S(2)}) async-start(), calls=%async_computation.20 | async-start | bytes 8028160
  995.9 445.5 %all-reduce.4.cloned.1.call-start = ((), (), s32[]{:S(2)}) async-start(), calls=%async_computation.23 | async-start | bytes 2359296 | tf_op jit(solution)/shard_map/psum | solution.py:283
  1038.8 31.2 %copy-start.2 = (bf16[2,784,4,64]{1,3,2,0:T(8,128)(2,1)S(1)}, bf16[2,784,4,64]{1,3,2,0:T(8,128)(2,1)}, u32[]{:S(2)}) copy-start(bf16[2,784,4,64]{1,3,2,0:T(8,128)(2,1)} %get-tuple-element.691) | copy-start | bytes 2408452 | tf_op jit(solution)/shard_map/while/body/eval_jaxpr/while
  1038.8 31.2 %copy-start.13 = (f32[1568,4,64]{0,2,1:T(8,128)S(1)}, f32[1568,4,64]{0,2,1:T(8,128)}, u32[]{:S(2)}) copy-start(f32[1568,4,64]{0,2,1:T(8,128)} %get-tuple-element.677) | copy-start | bytes 4816900 | tf_op jit(solution)/shard_map/while/body/eval_jaxpr/while
  1126.0 31.2 %copy-start.2 = (bf16[2,784,4,64]{1,3,2,0:T(8,128)(2,1)S(1)}, bf16[2,784,4,64]{1,3,2,0:T(8,128)(2,1)}, u32[]{:S(2)}) copy-start(bf16[2,784,4,64]{1,3,2,0:T(8,128)(2,1)} %get-tuple-element.691) | copy-start | bytes 2408452 | tf_op jit(solution)/shard_map/while/body/eval_jaxpr/while
  1126.0 31.2 %copy-start.13 = (f32[1568,4,64]{0,2,1:T(8,128)S(1)}, f32[1568,4,64]{0,2,1:T(8,128)}, u32[]{:S(2)}) copy-start(f32[1568,4,64]{0,2,1:T(8,128)} %get-tuple-element.677) | copy-start | bytes 4816900 | tf_op jit(solution)/shard_map/while/body/eval_jaxpr/while
  1232.5 31.2 %copy-start.2 = (bf16[2,784,4,64]{1,3,2,0:T(8,128)(2,1)S(1)}, bf16[2,784,4,64]{1,3,2,0:T(8,128)(2,1)}, u32[]{:S(2)}) copy-start(bf16[2,784,4,64]{1,3,2,0:T(8,128)(2,1)} %get-tuple-element.691) | copy-start | bytes 2408452 | tf_op jit(solution)/shard_map/while/body/eval_jaxpr/while
  1232.5 31.2 %copy-start.13 = (f32[1568,4,64]{0,2,1:T(8,128)S(1)}, f32[1568,4,64]{0,2,1:T(8,128)}, u32[]{:S(2)}) copy-start(f32[1568,4,64]{0,2,1:T(8,128)} %get-tuple-element.677) | copy-start | bytes 4816900 | tf_op jit(solution)/shard_map/while/body/eval_jaxpr/while
  1319.5 31.2 %copy-start.2 = (bf16[2,784,4,64]{1,3,2,0:T(8,128)(2,1)S(1)}, bf16[2,784,4,64]{1,3,2,0:T(8,128)(2,1)}, u32[]{:S(2)}) copy-start(bf16[2,784,4,64]{1,3,2,0:T(8,128)(2,1)} %get-tuple-element.691) | copy-start | bytes 2408452 | tf_op jit(solution)/shard_map/while/body/eval_jaxpr/while
  1319.5 31.2 %copy-start.13 = (f32[1568,4,64]{0,2,1:T(8,128)S(1)}, f32[1568,4,64]{0,2,1:T(8,128)}, u32[]{:S(2)}) copy-start(f32[1568,4,64]{0,2,1:T(8,128)} %get-tuple-element.677) | copy-start | bytes 4816900 | tf_op jit(solution)/shard_map/while/body/eval_jaxpr/while
  1397.3 72.2 %reduce-scatter.17.cloned.1.call-start = ((), (), s32[]{:S(2)}) async-start(), calls=%async_computation.15 | async-start | bytes 1966080 | tf_op jit(solution)/shard_map/reduce_scatter | solution.py:266
  1407.3 177.3 %reduce-scatter.31.cloned.1.call-start = ((), (), s32[]{:S(2)}) async-start(), calls=%async_computation.22 | async-start | bytes 8028160
  1482.2 108.0 %copy-start.5 = (bf16[2,392,1024]{2,1,0:T(8,128)(2,1)S(1)}, bf16[2,392,1024]{2,1,0:T(8,128)(2,1)}, u32[]{:S(2)}) copy-start(bf16[2,392,1024]{2,1,0:T(8,128)(2,1)} %param.24) | copy-start | bytes 4816900
  1482.2 108.0 %copy-start.36 = (f32[2,392]{1,0:T(2,128)S(1)}, f32[2,392]{1,0:T(2,128)}, u32[]{:S(2)}) copy-start(f32[2,392]{1,0:T(2,128)} %copy-done.35) | copy-start | bytes 9412
  1482.2 108.0 %copy-start.42 = (f32[1024]{0:T(1024)S(1)}, f32[1024]{0:T(1024)}, u32[]{:S(2)}) copy-start(f32[1024]{0:T(1024)} %copy-done.41) | copy-start | bytes 12292
  1482.2 108.0 %copy-start.44 = (f32[2,392]{1,0:T(2,128)S(1)}, f32[2,392]{1,0:T(2,128)}, u32[]{:S(2)}) copy-start(f32[2,392]{1,0:T(2,128)} %copy-done.43) | copy-start | bytes 9412
  1483.8 109.7 %copy-start.49 = (f32[1024]{0:T(1024)S(1)}, f32[1024]{0:T(1024)}, u32[]{:S(2)}) copy-start(f32[1024]{0:T(1024)} %get-tuple-element.386) | copy-start | bytes 12292
  1483.8 109.7 %copy-start.50 = (f32[1024]{0:T(1024)S(1)}, f32[1024]{0:T(1024)}, u32[]{:S(2)}) copy-start(f32[1024]{0:T(1024)} %get-tuple-element.306) | copy-start | bytes 12292
  1483.8 109.7 %copy-start.51 = (f32[1024]{0:T(1024)S(1)}, f32[1024]{0:T(1024)}, u32[]{:S(2)}) copy-start(f32[1024]{0:T(1024)} %get-tuple-element.312) | copy-start | bytes 12292
  1483.8 109.7 %copy-start.52 = (f32[1024]{0:T(1024)S(1)}, f32[1024]{0:T(1024)}, u32[]{:S(2)}) copy-start(f32[1024]{0:T(1024)} %get-tuple-element.388) | copy-start | bytes 12292
  1483.8 156.9 %copy-start.7 = (bf16[392,2,1024]{2,1,0:T(2,128)(2,1)S(1)}, bf16[392,2,1024]{2,1,0:T(2,128)(2,1)}, u32[]{:S(2)}) copy-start(bf16[392,2,1024]{2,1,0:T(2,128)(2,1)} %copy-done.6) | copy-start | bytes 4816900
  1483.8 156.9 %copy-start.31 = (f32[1024]{0:T(1024)S(1)}, f32[1024]{0:T(1024)}, u32[]{:S(2)}) copy-start(f32[1024]{0:T(1024)} %copy-done.30) | copy-start | bytes 12292
  1483.8 156.9 %copy-start.33 = (f32[2,392]{1,0:T(2,128)S(1)}, f32[2,392]{1,0:T(2,128)}, u32[]{:S(2)}) copy-start(f32[2,392]{1,0:T(2,128)} %copy-done.32) | copy-start | bytes 9412
  1483.8 156.9 %copy-start.38 = (f32[1024]{0:T(1024)S(1)}, f32[1024]{0:T(1024)}, u32[]{:S(2)}) copy-start(f32[1024]{0:T(1024)} %copy-done.37) | copy-start | bytes 12292
  1483.8 156.9 %copy-start.40 = (f32[2,392]{1,0:T(2,128)S(1)}, f32[2,392]{1,0:T(2,128)}, u32[]{:S(2)}) copy-start(f32[2,392]{1,0:T(2,128)} %copy-done.39) | copy-start | bytes 9412
  1483.8 156.9 %copy-start.46 = (f32[2,392]{1,0:T(2,128)S(1)}, f32[2,392]{1,0:T(2,128)}, u32[]{:S(2)}) copy-start(f32[2,392]{1,0:T(2,128)} %copy-done.45) | copy-start | bytes 9412
  1483.9 156.9 %copy-start.48 = (f32[2,392]{1,0:T(2,128)S(1)}, f32[2,392]{1,0:T(2,128)}, u32[]{:S(2)}) copy-start(f32[2,392]{1,0:T(2,128)} %copy-done.47) | copy-start | bytes 9412
  1483.9 156.9 %copy-start.54 = (f32[2]{0:T(128)S(1)}, f32[2]{0:T(128)}, u32[]{:S(2)}) copy-start(f32[2]{0:T(128)} %copy-done.53) | copy-start | bytes 28
  (56 other events, 224.8 us)
Sparse Core Ops, SparseCore 0:
  9.6 23.8 all-gather.10
  35.6 118.3 all-gather.8
  278.7 111.0 reduce-scatter.24
  391.2 23.0 all-gather.14
  416.3 117.4 all-gather.12
  535.2 21.0 all-gather.16
  557.9 117.4 all-gather.18
  717.3 111.0 reduce-scatter.28
  841.9 118.0 all-gather.20
  962.3 29.6 reduce-scatter.20
  994.6 31.4 reduce-scatter.22
  1029.0 21.6 reduce-scatter.18
  1053.1 112.8 reduce-scatter.26
  1397.4 41.3 all-reduce.3
  1441.2 28.1 reduce-scatter.16
  1471.8 112.8 reduce-scatter.30
